TPU v7x, 128 devices: a whole 4x4x4 slice. The times are simulated.
128 devices in a mesh: grid: 16 (over y, z), blk: 8 (over x, core).
Axes of the slice: x: 4, y: 4, z: 4, core: 2. Of those that a mesh axis runs over, the one named last changes fastest.
Arguments:
- a_slots: bfloat16 [16, 8, 16, 2, 128, 128], P('grid', 'blk'), may hold values from -6 to 6
- a_rows: int32 [16, 8, 16, 2], P('grid', 'blk'), may hold values from 0 to 127, as said below
- a_cols: int32 [16, 8, 16, 2], P('grid', 'blk'), may hold values from 0 to 63
- a_count: int32 [16, 8, 16], P('grid', 'blk'), may hold values from 0 to 2, as said below
- owned_rows: int32 [16, 8], P('grid'), may hold values from 0 to 127, as said below
- b_matrix: bfloat16 [8192, 8192], P('grid', 'blk'), may hold values from -0.125 to 0.125
Outputs:
- product: bfloat16 [16384, 8192], P('grid', 'blk')
Inputs may be any that keep to these rules, and one draw needn't show every extreme that they name: `a_rows`: every slot sent to product owner g, live or padded, names one of the block rows owned_rows[g, 0 .. 7]; no two slots of the whole draw name the same block row and block column. `a_count`: some product owner receives 2 live slots from every atom owner and atom column. `owned_rows`: A permutation of the 128 block rows.
All inputs are finite; a program needn't handle non-finite values.
Results may differ from a plain program's by a relative error of at most 0.001.
Values may be sent and summed in bfloat16 or wider, within the bound.
A program may use at most 128 MiB of HBM per device.

v0:
```python
import jax
import jax.numpy as jnp
from jax import lax
from jax.sharding import PartitionSpec as P

CAP = 2
RB = 8


def body(a_slots, a_rows, a_cols, a_count, owned_rows, b_matrix):
    groups = lax.axis_size("grid")
    columns = lax.axis_size("blk")
    block_size = a_slots.shape[-1]
    landed = (
        lax.all_to_all(
            a_slots.reshape(groups, CAP, block_size, block_size),
            "grid",
            split_axis=0,
            concat_axis=0,
            tiled=True,
        ),
        lax.all_to_all(
            a_rows.reshape(groups, CAP), "grid", split_axis=0, concat_axis=0, tiled=True
        ),
        lax.all_to_all(
            a_cols.reshape(groups, CAP), "grid", split_axis=0, concat_axis=0, tiled=True
        ),
        lax.all_to_all(a_count.reshape(groups, 1), "grid", split_axis=0, concat_axis=0, tiled=True),
    )
    slot_data, slot_rows, slot_cols, slot_count = (
        lax.all_gather(landed[0][None], "blk", axis=0, tiled=True),
        lax.all_gather(landed[1][None], "blk", axis=0, tiled=True),
        lax.all_gather(landed[2][None], "blk", axis=0, tiled=True),
        lax.all_gather(landed[3][None], "blk", axis=0, tiled=True),
    )
    total = columns * groups * CAP
    live = (jnp.arange(CAP, dtype=jnp.int32)[None, None, :] < slot_count).reshape(total)
    slot_rows = slot_rows.reshape(total)
    slot_cols = slot_cols.reshape(total)
    slot_data = slot_data.reshape(total, block_size, block_size)
    owned = owned_rows.reshape(RB)
    row_hit = (slot_rows[:, None] == owned[None, :]) & live[:, None]
    k_blocks = b_matrix.shape[0] * groups // block_size
    col_hit = slot_cols[:, None] == jnp.arange(k_blocks, dtype=jnp.int32)[None, :]
    placing = (
        (row_hit[:, :, None] & col_hit[:, None, :])
        .reshape(total, RB * k_blocks)
        .astype(jnp.bfloat16)
    )
    spread = jnp.einsum(
        "sp,sq->pq",
        placing,
        slot_data.reshape(total, block_size * block_size),
        preferred_element_type=jnp.float32,
    )
    tile = spread.astype(jnp.bfloat16).reshape(RB, k_blocks, block_size, block_size)
    tile = tile.transpose(0, 2, 1, 3).reshape(RB * block_size, k_blocks * block_size)
    result = jnp.dot(
        tile,
        lax.all_gather(b_matrix, "grid", axis=0, tiled=True),
        preferred_element_type=jnp.float32,
    )
    return result.astype(jnp.bfloat16)


def solution(mesh):
    in_specs = (
        P("grid", "blk", None, None, None, None),
        P("grid", "blk", None, None),
        P("grid", "blk", None, None),
        P("grid", "blk", None),
        P("grid", None),
        P("grid", "blk"),
    )
    out_specs = P("grid", "blk")
    return jax.shard_map(body, mesh=mesh, in_specs=in_specs, out_specs=out_specs, check_vma=False)
```

profile of v0, /device:TPU:1, one launch (start us, length us, event | category | flops | bytes accessed | tf_op | source)
XLA Modules:
  0.0 225.2 jit_solution(14155272657976014603)
XLA Ops:
  6.5 0.0 all-gather.9.cloned.1.call-start
  6.5 24.6 %all_to_all.32 = bf16[16,2,128,128]{3,2,1,0:T(8,128)(2,1)} all-to-all(bf16[16,2,128,128]{3,2,1,0:T(8,128)(2,1)} %bitcast.31), channel_id=1, replica_groups=mesh['grid'=16,'blk'=8] {'grid'}, dimensions={0} | all-to-all | bytes 2097152 | tf_op jit(solution)/shard_map/all_to_all | solution.py:15
  31.1 0.0 all-gather.9.cloned.1.call-update
  31.1 0.0 all-gather.7.cloned.1.call-start
  31.2 0.7 all-gather.7.cloned.1.call-update
  31.9 1.3 copy.15
  33.2 3.6 %all-to-all-start.1 = ((s32[16,1,1]{2,1,0:T(1,128)}), s32[16,1,1]{2,1,0:T(1,128)S(1)}, u32[]{:S(2)}, u32[]{:S(2)}) async-start(s32[16,1,1]{2,1,0:T(1,128)} %copy.15), calls=%async_computation.1 | async-start | bytes 16384 | tf_op jit(solution)/shard_map/all_to_all | solution.py:28
  36.9 1.3 copy.14
  38.2 1.4 copy.16
  39.6 1.3 dynamic-slice
  41.5 1.8 all-to-all-done.1
  43.3 4.9 %all-to-all-start = ((s32[16,1,2]{2,1,0:T(1,128)}), s32[16,1,2]{2,1,0:T(1,128)S(1)}, u32[]{:S(2)}, u32[]{:S(2)}) async-start(s32[16,1,2]{2,1,0:T(1,128)} %copy.14), calls=%async_computation | async-start | bytes 16384 | tf_op jit(solution)/shard_map/all_to_all | solution.py:22
  48.1 0.4 reduce.1
  48.5 0.2 dynamic-update-slice
  48.8 10.3 %all-reduce = s32[128]{0:T(128)S(1)} all-reduce(s32[128]{0:T(128)S(1)} %dynamic-update-slice), channel_id=3, replica_groups=mesh['grid'=16,'blk'=8] {'blk'}, use_global_device_ids=true, to_apply=%add | all-reduce | flops 128 | bytes 1024
  59.1 0.1 lt.23
  59.1 0.1 iota_compare_fusion.1
  59.2 0.1 lt.26
  59.4 0.0 all-to-all-done
  59.4 6.9 %all-to-all-start.2 = ((s32[16,1,2]{2,1,0:T(1,128)}), s32[16,1,2]{2,1,0:T(1,128)S(1)}, u32[]{:S(2)}, u32[]{:S(2)}) async-start(s32[16,1,2]{2,1,0:T(1,128)} %copy.16), calls=%async_computation.2 | async-start | bytes 16384 | tf_op jit(solution)/shard_map/all_to_all | solution.py:25
  66.3 14.7 %all-gather = s32[128,1,2]{2,1,0:T(1,128)S(1)} all-gather(s32[16,1,2]{2,1,0:T(1,128)S(1)} %all-to-all-done), channel_id=2, replica_groups=mesh['grid'=16,'blk'=8] {'blk'}, dimensions={0}, use_global_device_ids=true | all-gather | bytes 1152 | tf_op jit(solution)/shard_map/all_gather | solution.py:32
  81.0 0.6 broadcast.56
  81.6 0.8 reduce.8
  82.5 0.1 eq.40
  82.6 0.0 all-to-all-done.2
  82.6 12.8 %all-gather.2 = s32[128,1,2]{2,1,0:T(1,128)S(1)} all-gather(s32[16,1,2]{2,1,0:T(1,128)S(1)} %all-to-all-done.2), channel_id=4, replica_groups=mesh['grid'=16,'blk'=8] {'blk'}, dimensions={0}, use_global_device_ids=true | all-gather | bytes 1152 | tf_op jit(solution)/shard_map/all_gather | solution.py:33
  95.4 0.9 reduce.7
  96.2 0.1 eq.45
  96.4 0.7 compare_and_fusion
  97.1 0.1 broadcast_and_fusion
  97.2 0.0 all-gather.9.cloned.1.call-done
  97.2 18.5 %fusion.5 = bf16[64,8,128,128]{3,1,2,0:T(8,128)(2,1)} fusion(pred[256,512]{0,1:T(32,128)(4,1)S(1)} %bitcast.32, bf16[32,8,128,128]{3,2,1,0:T(8,128)(2,1)} %bitcast.30), kind=kOutput, calls=%fused_computation.6 | convolution fusion | flops 4303355904 | bytes 25296896 | tf_op jit(solution)/shard_map/sp,sq->pq/dot_general | solution.py:50
  115.7 10.4 %copy.19 = bf16[64,8,128,128]{3,2,1,0:T(8,128)(2,1)S(1)} copy(bf16[64,8,128,128]{3,1,2,0:T(8,128)(2,1)} %fusion.5) | data formatting | bytes 33554432
  126.1 11.8 %copy.17 = bf16[8,64,128,128]{3,1,2,0:T(8,128)(2,1)} copy(bf16[8,64,128,128]{3,2,1,0:T(8,128)(2,1)S(1)} %bitcast.28) | data formatting | bytes 33554432 | tf_op jit(solution)/shard_map/reshape | solution.py:56
  138.0 56.6 %all-gather.7.cloned.1.call-done = bf16[8192,1024]{1,0:T(8,128)(2,1)} async-done(((bf16[512,1024]{1,0:T(8,128)(2,1)}), bf16[8192,1024]{1,0:T(8,128)(2,1)}) %all-gather.7.cloned.1.call-update) | async-done | bytes 16777232 | tf_op jit(solution)/shard_map/all_gather | solution.py:60
  194.6 23.8 %fusion.8 = bf16[1024,1024]{1,0:T(8,128)(2,1)} fusion(bf16[8192,1024]{1,0:T(8,128)(2,1)} %all-gather.7.cloned.1.call-done, bf16[128,8,64,128]{3,2,1,0:T(8,128)(2,1)} %bitcast.29), kind=kOutput, calls=%fused_computation.7 | convolution fusion | flops 17180917760 | bytes 35651584 | tf_op jit(solution)/shard_map/dot_general | solution.py:58
  (2 shorter events, 0.0 us)
Async XLA Ops:
  6.5 90.7 %all-gather.9.cloned.1.call-start = ((), (), s32[]{:S(2)}) async-start(), calls=%async_computation.5 | async-start | bytes 9437184 | tf_op jit(solution)/shard_map/all_gather | solution.py:31
  31.1 163.5 %all-gather.7.cloned.1.call-start = ((), (), s32[]{:S(2)}) async-start(), calls=%async_computation.4 | async-start | bytes 17825792 | tf_op jit(solution)/shard_map/all_gather | solution.py:60
  33.2 10.0 %all-to-all-start.1 = ((s32[16,1,1]{2,1,0:T(1,128)}), s32[16,1,1]{2,1,0:T(1,128)S(1)}, u32[]{:S(2)}, u32[]{:S(2)}) async-start(s32[16,1,1]{2,1,0:T(1,128)} %copy.15), calls=%async_computation.1 | async-start | bytes 16384 | tf_op jit(solution)/shard_map/all_to_all | solution.py:28
  43.3 16.1 %all-to-all-start = ((s32[16,1,2]{2,1,0:T(1,128)}), s32[16,1,2]{2,1,0:T(1,128)S(1)}, u32[]{:S(2)}, u32[]{:S(2)}) async-start(s32[16,1,2]{2,1,0:T(1,128)} %copy.14), calls=%async_computation | async-start | bytes 16384 | tf_op jit(solution)/shard_map/all_to_all | solution.py:22
  59.4 23.2 %all-to-all-start.2 = ((s32[16,1,2]{2,1,0:T(1,128)}), s32[16,1,2]{2,1,0:T(1,128)S(1)}, u32[]{:S(2)}, u32[]{:S(2)}) async-start(s32[16,1,2]{2,1,0:T(1,128)} %copy.16), calls=%async_computation.2 | async-start | bytes 16384 | tf_op jit(solution)/shard_map/all_to_all | solution.py:25
Sparse Core Ops, SparseCore 0:
  31.3 49.8 all-gather.8
  83.3 111.2 all-gather.6
where the time goes:
time: 226 us; the launch traced here: 225 us
  blocking collectives  62.3 us (28%)
  waiting for transfers between devices  59.1 us (26%)
  matrix products  42.3 us (19%)
  local copies, waits for them, and re-layouts  28.9 us (13%)
  starting transfers between devices  15.5 us (7%)
  between operations  14.2 us (6%)
  other arithmetic  2.97 us (1%)
    all_gather x1, waiting for transfers between devices, body(): lax.all_gather(b_matrix, 'grid', axis=0, tiled=True)  56.6 us
    all_to_all x1, blocking collectives, body(): lax.all_to_all(a_slots.reshape(groups, CAP, block_size, block_size), 'gri...  24.6 us
    dot_general x1, matrix products, body(): jnp.dot(tile, lax.all_gather(b_matrix, 'grid', axis=0, tiled=True), prefe...  23.8 us
    dot_general x1, matrix products, body(): jnp.einsum('sp,sq->pq', placing, slot_data.reshape(total, block_size * bl...  18.5 us
    all_gather x1, blocking collectives, body(): lax.all_gather(landed[1][None], 'blk', axis=0, tiled=True)  14.7 us
    all_gather x1, blocking collectives, body(): lax.all_gather(landed[2][None], 'blk', axis=0, tiled=True)  12.8 us
    unnamed x4, local copies, waits for them, and re-layouts  11.9 us
    reshape x1, local copies, waits for them, and re-layouts, body(): spread.astype(jnp.bfloat16).reshape(RB, k_blocks, block_size, block_size)  11.8 us
  transfers between devices with their start and end apart: 5, of which 2 were waited for; matrix products, arithmetic and copies ran while one was open for 22% of the time, Pallas kernels for 0%

commit v1 on v0

--- a/solution.py
+++ b/solution.py
@@ -5,6 +5,27 @@
 
 CAP = 2
 RB = 8
+
+
+def ring_gather(x, axis, dim):
+    count, place, rows = (lax.axis_size(axis), lax.axis_index(axis), x.shape[dim])
+    upward = [(i, (i + 1) % count) for i in range(count)]
+    left = [(i, (i - 1) % count) for i in range(count)]
+    out = jnp.zeros((*x.shape[:dim], count * rows, *x.shape[dim + 1 :]), x.dtype)
+    out = lax.dynamic_update_slice_in_dim(out, x, place * rows, axis=dim)
+    from_left = from_right = x
+    halfway = count // 2
+    for step in range(1, halfway + 1):
+        from_left = lax.ppermute(from_left, axis, upward)
+        out = lax.dynamic_update_slice_in_dim(
+            out, from_left, (place - step) % count * rows, axis=dim
+        )
+        if step < count - halfway:
+            from_right = lax.ppermute(from_right, axis, left)
+            out = lax.dynamic_update_slice_in_dim(
+                out, from_right, (place + step) % count * rows, axis=dim
+            )
+    return out
 
 
 def body(a_slots, a_rows, a_cols, a_count, owned_rows, b_matrix):
@@ -55,11 +76,7 @@
     )
     tile = spread.astype(jnp.bfloat16).reshape(RB, k_blocks, block_size, block_size)
     tile = tile.transpose(0, 2, 1, 3).reshape(RB * block_size, k_blocks * block_size)
-    result = jnp.dot(
-        tile,
-        lax.all_gather(b_matrix, "grid", axis=0, tiled=True),
-        preferred_element_type=jnp.float32,
-    )
+    result = jnp.dot(tile, ring_gather(b_matrix, "grid", 0), preferred_element_type=jnp.float32)
     return result.astype(jnp.bfloat16)
 
 

time: 226 us -> 410 us (1.81)
  waiting for transfers between devices: 59.1 us -> 125 us
  local copies, waits for them, and re-layouts: 28.9 us -> 88.7 us
  starting transfers between devices: 15.5 us -> 51.3 us
  matrix products: 42.3 us -> 59.1 us
  blocking collectives: 62.3 us -> 67.5 us
    ppermute x0 -> x15, waiting for transfers between devices: none -> 123 us  [the longest x8 104 us: ring_gather(): from_left = lax.ppermute(from_left, axis, upward)]
    all_gather x1 -> x0, waiting for transfers between devices: 56.6 us -> none  [body(): lax.all_gather(b_matrix, 'grid', axis=0, tiled=True)]
    ppermute x0 -> x15, starting transfers between devices: none -> 34.4 us  [the longest x7 33.8 us: ring_gather(): from_right = lax.ppermute(from_right, axis, left)]
    dynamic_update_slice x0 -> x16, local copies, waits for them, and re-layouts: none -> 28 us  [the longest x8 14.6 us: ring_gather(): lax.dynamic_update_slice_in_dim(out, from_left, (place - step) % count *...]
    reshape x1, local copies, waits for them, and re-layouts: 11.8 us -> 37.2 us  [body(): spread.astype(jnp.bfloat16).reshape(RB, k_blocks, block_size, block_size)]
    dot_general x1, matrix products: 23.8 us -> 40.8 us  [body(): jnp.dot(tile, ring_gather(b_matrix, 'grid', 0), preferred_element_type=jn...]
    broadcast_in_dim x0 -> x1, local copies, waits for them, and re-layouts: none -> 6 us  [ring_gather(): out = jnp.zeros((*x.shape[:dim], count * rows, *x.shape[dim + 1:]), x.dtype)]
    unnamed x1, blocking collectives: 10.3 us -> 15 us
  transfers between devices with their start and end apart: 5 -> 19, of which waited for: 2 -> 9; matrix products, arithmetic and copies ran while one was open for 22% -> 11% of each run, Pallas kernels for 0% -> 0%
where the time goes in v1:
time: 410 us; the launch traced here: 409 us
  waiting for transfers between devices  125 us (30%)
  local copies, waits for them, and re-layouts  88.7 us (22%)
  blocking collectives  67.5 us (16%)
  matrix products  59.1 us (14%)
  starting transfers between devices  51.3 us (13%)
  between operations  14.5 us (4%)
    ppermute x8, waiting for transfers between devices, ring_gather(): from_left = lax.ppermute(from_left, axis, upward)  104 us
    dot_general x1, matrix products, body(): jnp.dot(tile, ring_gather(b_matrix, 'grid', 0), preferred_element_type=jn...  40.8 us
    reshape x1, local copies, waits for them, and re-layouts, body(): spread.astype(jnp.bfloat16).reshape(RB, k_blocks, block_size, block_size)  37.2 us
    ppermute x7, starting transfers between devices, ring_gather(): from_right = lax.ppermute(from_right, axis, left)  33.8 us
    all_to_all x1, blocking collectives, body(): lax.all_to_all(a_slots.reshape(groups, CAP, block_size, block_size), 'gri...  24.7 us
    ppermute x7, waiting for transfers between devices, ring_gather(): from_right = lax.ppermute(from_right, axis, left)  19.2 us
    dot_general x1, matrix products, body(): jnp.einsum('sp,sq->pq', placing, slot_data.reshape(total, block_size * bl...  18.3 us
    all_gather x1, blocking collectives, body(): lax.all_gather(landed[1][None], 'blk', axis=0, tiled=True)  15.1 us
  transfers between devices with their start and end apart: 19, of which 9 were waited for; matrix products, arithmetic and copies ran while one was open for 11% of the time, Pallas kernels for 0%

profile of v1, /device:TPU:1, one launch (start us, length us, event | category | flops | bytes accessed | tf_op | source)
XLA Modules:
  0.0 408.7 jit_solution(436560443606345604)
XLA Ops:
  6.5 24.7 %all_to_all.32 = bf16[16,2,128,128]{3,2,1,0:T(8,128)(2,1)} all-to-all(bf16[16,2,128,128]{3,2,1,0:T(8,128)(2,1)} %bitcast.31), channel_id=1, replica_groups=mesh['grid'=16,'blk'=8] {'grid'}, dimensions={0} | all-to-all | bytes 2097152 | tf_op jit(solution)/shard_map/all_to_all | solution.py:36
  31.9 4.2 %collective-permute-start.1 = (bf16[512,1024]{1,0:T(8,128)(2,1)}, bf16[512,1024]{1,0:T(8,128)(2,1)S(1)}, u32[]{:S(2)}, u32[]{:S(2)}) collective-permute-start(bf16[512,1024]{1,0:T(8,128)(2,1)} %param.11), channel_id=1, source_target_pairs={{0,120},{8,0},{16,8},{24,16},{32,24},{40,32},{48,40},{56,48},{64,5... | collective-permute-start | bytes 3145736 | tf_op jit(solution)/shard_map/ppermute | solution.py:24
  36.1 21.5 %collective-permute-done = bf16[512,1024]{1,0:T(8,128)(2,1)S(1)} collective-permute-done((bf16[512,1024]{1,0:T(8,128)(2,1)}, bf16[512,1024]{1,0:T(8,128)(2,1)S(1)}, u32[]{:S(2)}, u32[]{:S(2)}) %collective-permute-start) | collective-permute-done | bytes 1048608 | tf_op jit(solution)/shard_map/ppermute | solution.py:19
  57.6 4.8 %collective-permute-start.3 = (bf16[512,1024]{1,0:T(8,128)(2,1)S(1)}, bf16[512,1024]{1,0:T(8,128)(2,1)S(1)}, u32[]{:S(2)}, u32[]{:S(2)}) collective-permute-start(bf16[512,1024]{1,0:T(8,128)(2,1)S(1)} %collective-permute-done.1), channel_id=1, source_target_pairs={{0,120},{8,0},{16,8},{24,16},{32,24},{40,32},{48,40},{56,48},{64,5... | collective-permute-start | bytes 3145736 | tf_op jit(solution)/shard_map/ppermute | solution.py:24
  62.4 20.3 %collective-permute-done.2 = bf16[512,1024]{1,0:T(8,128)(2,1)S(1)} collective-permute-done((bf16[512,1024]{1,0:T(8,128)(2,1)S(1)}, bf16[512,1024]{1,0:T(8,128)(2,1)S(1)}, u32[]{:S(2)}, u32[]{:S(2)}) %collective-permute-start.2) | collective-permute-done | bytes 1048608 | tf_op jit(solution)/shard_map/ppermute | solution.py:19
  82.7 4.8 %collective-permute-start.5 = (bf16[512,1024]{1,0:T(8,128)(2,1)S(1)}, bf16[512,1024]{1,0:T(8,128)(2,1)S(1)}, u32[]{:S(2)}, u32[]{:S(2)}) collective-permute-start(bf16[512,1024]{1,0:T(8,128)(2,1)S(1)} %collective-permute-done.3), channel_id=1, source_target_pairs={{0,120},{8,0},{16,8},{24,16},{32,24},{40,32},{48,40},{56,48},{64,5... | collective-permute-start | bytes 3145736 | tf_op jit(solution)/shard_map/ppermute | solution.py:24
  87.5 19.4 %collective-permute-done.4 = bf16[512,1024]{1,0:T(8,128)(2,1)S(1)} collective-permute-done((bf16[512,1024]{1,0:T(8,128)(2,1)S(1)}, bf16[512,1024]{1,0:T(8,128)(2,1)S(1)}, u32[]{:S(2)}, u32[]{:S(2)}) %collective-permute-start.4) | collective-permute-done | bytes 1048608 | tf_op jit(solution)/shard_map/ppermute | solution.py:19
  106.9 4.8 %collective-permute-start.7 = (bf16[512,1024]{1,0:T(8,128)(2,1)S(1)}, bf16[512,1024]{1,0:T(8,128)(2,1)}, u32[]{:S(2)}, u32[]{:S(2)}) collective-permute-start(bf16[512,1024]{1,0:T(8,128)(2,1)S(1)} %collective-permute-done.5), channel_id=1, source_target_pairs={{0,120},{8,0},{16,8},{24,16},{32,24},{40,32},{48,40},{56,48},{64,5... | collective-permute-start | bytes 3145736 | tf_op jit(solution)/shard_map/ppermute | solution.py:24
  111.7 18.5 %collective-permute-done.6 = bf16[512,1024]{1,0:T(8,128)(2,1)S(1)} collective-permute-done((bf16[512,1024]{1,0:T(8,128)(2,1)S(1)}, bf16[512,1024]{1,0:T(8,128)(2,1)S(1)}, u32[]{:S(2)}, u32[]{:S(2)}) %collective-permute-start.6) | collective-permute-done | bytes 1048608 | tf_op jit(solution)/shard_map/ppermute | solution.py:19
  131.2 4.8 %collective-permute-start.9 = (bf16[512,1024]{1,0:T(8,128)(2,1)}, bf16[512,1024]{1,0:T(8,128)(2,1)}, u32[]{:S(2)}, u32[]{:S(2)}) collective-permute-start(bf16[512,1024]{1,0:T(8,128)(2,1)} %collective-permute-done.7), channel_id=1, source_target_pairs={{0,120},{8,0},{16,8},{24,16},{32,24},{40,32},{48,40},{56,48},{64,5... | collective-permute-start | bytes 3145736 | tf_op jit(solution)/shard_map/ppermute | solution.py:24
  136.0 17.7 %collective-permute-done.8 = bf16[512,1024]{1,0:T(8,128)(2,1)} collective-permute-done((bf16[512,1024]{1,0:T(8,128)(2,1)S(1)}, bf16[512,1024]{1,0:T(8,128)(2,1)}, u32[]{:S(2)}, u32[]{:S(2)}) %collective-permute-start.8) | collective-permute-done | bytes 1048608 | tf_op jit(solution)/shard_map/ppermute | solution.py:19
  153.7 1.3 copy.15
  155.0 6.2 %all-to-all-start.1 = ((s32[16,1,1]{2,1,0:T(1,128)}), s32[16,1,1]{2,1,0:T(1,128)S(1)}, u32[]{:S(2)}, u32[]{:S(2)}) async-start(s32[16,1,1]{2,1,0:T(1,128)} %copy.15), calls=%async_computation.1 | async-start | bytes 16384 | tf_op jit(solution)/shard_map/all_to_all | solution.py:49
  161.4 1.4 copy.14
  162.8 1.3 copy.16
  164.1 1.3 dynamic-slice
  165.4 6.0 %broadcast_in_dim.23 = bf16[8192,1024]{1,0:T(8,128)(2,1)} broadcast(bf16[]{:T(256)} %constant.90.clone.1), dimensions={} | broadcast | bytes 16777218 | tf_op jit(solution)/shard_map/broadcast_in_dim | solution.py:14
  171.4 1.0 constant_dynamic-update-slice_fusion.15
  173.1 2.4 all-to-all-done.1
  175.4 4.0 all-to-all-start
  180.1 15.0 %all-reduce = s32[128]{0:T(128)S(1)} all-reduce(s32[128]{0:T(128)S(1)} %dynamic-update-slice), channel_id=3, replica_groups=mesh['grid'=16,'blk'=8] {'blk'}, use_global_device_ids=true, to_apply=%add | all-reduce | flops 128 | bytes 1024
  195.4 6.7 %all-to-all-start.2 = ((s32[16,1,2]{2,1,0:T(1,128)}), s32[16,1,2]{2,1,0:T(1,128)S(1)}, u32[]{:S(2)}, u32[]{:S(2)}) async-start(s32[16,1,2]{2,1,0:T(1,128)} %copy.16), calls=%async_computation.2 | async-start | bytes 16384 | tf_op jit(solution)/shard_map/all_to_all | solution.py:46
  202.1 15.1 %all-gather = s32[128,1,2]{2,1,0:T(1,128)S(1)} all-gather(s32[16,1,2]{2,1,0:T(1,128)S(1)} %all-to-all-done), channel_id=2, replica_groups=mesh['grid'=16,'blk'=8] {'blk'}, dimensions={0}, use_global_device_ids=true | all-gather | bytes 1152 | tf_op jit(solution)/shard_map/all_gather | solution.py:53
  218.7 12.8 %all-gather.2 = s32[128,1,2]{2,1,0:T(1,128)S(1)} all-gather(s32[16,1,2]{2,1,0:T(1,128)S(1)} %all-to-all-done.2), channel_id=4, replica_groups=mesh['grid'=16,'blk'=8] {'blk'}, dimensions={0}, use_global_device_ids=true | all-gather | bytes 1152 | tf_op jit(solution)/shard_map/all_gather | solution.py:54
  232.5 5.0 %collective-permute-start.11 = (bf16[512,1024]{1,0:T(8,128)(2,1)}, bf16[512,1024]{1,0:T(8,128)(2,1)S(1)}, u32[]{:S(2)}, u32[]{:S(2)}) collective-permute-start(bf16[512,1024]{1,0:T(8,128)(2,1)} %collective-permute-done.9), channel_id=1, source_target_pairs={{0,120},{8,0},{16,8},{24,16},{32,24},{40,32},{48,40},{56,48},{64,5... | collective-permute-start | bytes 3145736 | tf_op jit(solution)/shard_map/ppermute | solution.py:24
  237.7 1.1 constant_dynamic-update-slice_fusion.14
  238.8 1.1 constant_dynamic-update-slice_fusion.13
  239.8 2.3 constant_dynamic-update-slice_fusion.12
  242.1 2.3 constant_dynamic-update-slice_fusion.11
  244.3 2.3 constant_dynamic-update-slice_fusion.10
  246.6 13.6 %collective-permute-done.11 = bf16[512,1024]{1,0:T(8,128)(2,1)S(1)} collective-permute-done((bf16[512,1024]{1,0:T(8,128)(2,1)}, bf16[512,1024]{1,0:T(8,128)(2,1)S(1)}, u32[]{:S(2)}, u32[]{:S(2)}) %collective-permute-start.11) | collective-permute-done | bytes 1048608 | tf_op jit(solution)/shard_map/ppermute | solution.py:24
  260.2 5.4 %collective-permute-start.13 = (bf16[512,1024]{1,0:T(8,128)(2,1)S(1)}, bf16[512,1024]{1,0:T(8,128)(2,1)S(1)}, u32[]{:S(2)}, u32[]{:S(2)}) collective-permute-start(bf16[512,1024]{1,0:T(8,128)(2,1)S(1)} %collective-permute-done.11), channel_id=1, source_target_pairs={{0,120},{8,0},{16,8},{24,16},{32,24},{40,32},{48,40},{56,48},{64,5... | collective-permute-start | bytes 3145736 | tf_op jit(solution)/shard_map/ppermute | solution.py:24
  265.6 2.3 constant_dynamic-update-slice_fusion.9
  267.9 2.3 constant_dynamic-update-slice_fusion.8
  270.3 2.3 constant_dynamic-update-slice_fusion.7
  272.5 2.3 constant_dynamic-update-slice_fusion.6
  274.8 2.3 constant_dynamic-update-slice_fusion.5
  277.1 2.3 constant_dynamic-update-slice_fusion.4
  279.4 1.0 constant_dynamic-update-slice_fusion.3
  280.4 1.1 constant_dynamic-update-slice_fusion.2
  281.5 5.6 %collective-permute-done.13 = bf16[512,1024]{1,0:T(8,128)(2,1)S(1)} collective-permute-done((bf16[512,1024]{1,0:T(8,128)(2,1)S(1)}, bf16[512,1024]{1,0:T(8,128)(2,1)S(1)}, u32[]{:S(2)}, u32[]{:S(2)}) %collective-permute-start.13) | collective-permute-done | bytes 1048608 | tf_op jit(solution)/shard_map/ppermute | solution.py:24
  287.1 1.1 constant_dynamic-update-slice_fusion.1
  288.2 6.4 %collective-permute-done.14 = bf16[512,1024]{1,0:T(8,128)(2,1)S(1)} collective-permute-done((bf16[512,1024]{1,0:T(8,128)(2,1)S(1)}, bf16[512,1024]{1,0:T(8,128)(2,1)S(1)}, u32[]{:S(2)}, u32[]{:S(2)}) %collective-permute-start.14) | collective-permute-done | bytes 1048608 | tf_op jit(solution)/shard_map/ppermute | solution.py:19
  294.6 1.1 constant_dynamic-update-slice_fusion
  295.8 18.3 %fusion.5 = bf16[64,8,128,128]{3,1,2,0:T(8,128)(2,1)} fusion(pred[256,512]{0,1:T(32,128)(4,1)S(1)} %bitcast.32, bf16[32,8,128,128]{3,2,1,0:T(8,128)(2,1)} %bitcast.30), kind=kOutput, calls=%fused_computation.6 | convolution fusion | flops 4303355904 | bytes 25296896 | tf_op jit(solution)/shard_map/sp,sq->pq/dot_general | solution.py:71
  314.1 9.8 %copy.19 = bf16[64,8,128,128]{3,2,1,0:T(8,128)(2,1)S(1)} copy(bf16[64,8,128,128]{3,1,2,0:T(8,128)(2,1)} %fusion.5) | data formatting | bytes 33554432
  323.9 37.2 %copy.17 = bf16[8,64,128,128]{3,1,2,0:T(8,128)(2,1)S(1)} copy(bf16[8,64,128,128]{3,2,1,0:T(8,128)(2,1)S(1)} %bitcast.28) | data formatting | bytes 33554432 | tf_op jit(solution)/shard_map/reshape | solution.py:77
  361.1 40.8 %fusion.8 = bf16[1024,1024]{1,0:T(8,128)(2,1)} fusion(bf16[8192,1024]{1,0:T(8,128)(2,1)} %constant_dynamic-update-slice_fusion, bf16[128,8,64,128]{3,2,1,0:T(8,128)(2,1)S(1)} %bitcast.29), kind=kOutput, calls=%fused_computation.7 | convolution fusion | flops 17180917760 | bytes 35651584 | tf_op jit(solution)/shard_map/dot_general | solution.py:79
  (48 shorter events, 5.4 us)
Async XLA Ops:
  6.5 164.9 %copy-start = (bf16[512,1024]{1,0:T(8,128)(2,1)S(1)}, bf16[512,1024]{1,0:T(8,128)(2,1)}, u32[]{:S(2)}) copy-start(bf16[512,1024]{1,0:T(8,128)(2,1)} %param.11) | copy-start | bytes 3145732
  6.5 231.0 %copy-start.6 = (s32[1,8]{1,0:T(1,128)S(1)}, s32[1,8]{1,0:T(1,128)}, u32[]{:S(2)}) copy-start(s32[1,8]{1,0:T(1,128)} %param.10) | copy-start | bytes 100
  6.5 289.2 %all-gather.6.cloned.1.call-start = ((), (), s32[]{:S(2)}) async-start(), calls=%async_computation.4 | async-start | bytes 9437184 | tf_op jit(solution)/shard_map/all_gather | solution.py:52
  31.3 26.3 %collective-permute-start = (bf16[512,1024]{1,0:T(8,128)(2,1)}, bf16[512,1024]{1,0:T(8,128)(2,1)S(1)}, u32[]{:S(2)}, u32[]{:S(2)}) collective-permute-start(bf16[512,1024]{1,0:T(8,128)(2,1)} %param.11), channel_id=1, source_target_pairs={{0,8},{8,16},{16,24},{24,32},{32,40},{40,48},{48,56},{56,64},{64,7... | collective-permute-start | bytes 3145736 | tf_op jit(solution)/shard_map/ppermute | solution.py:19
  31.9 25.7 %collective-permute-start.1 = (bf16[512,1024]{1,0:T(8,128)(2,1)}, bf16[512,1024]{1,0:T(8,128)(2,1)S(1)}, u32[]{:S(2)}, u32[]{:S(2)}) collective-permute-start(bf16[512,1024]{1,0:T(8,128)(2,1)} %param.11), channel_id=1, source_target_pairs={{0,120},{8,0},{16,8},{24,16},{32,24},{40,32},{48,40},{56,48},{64,5... | collective-permute-start | bytes 3145736 | tf_op jit(solution)/shard_map/ppermute | solution.py:24
  57.6 25.1 %collective-permute-start.2 = (bf16[512,1024]{1,0:T(8,128)(2,1)S(1)}, bf16[512,1024]{1,0:T(8,128)(2,1)S(1)}, u32[]{:S(2)}, u32[]{:S(2)}) collective-permute-start(bf16[512,1024]{1,0:T(8,128)(2,1)S(1)} %collective-permute-done), channel_id=1, source_target_pairs={{0,8},{8,16},{16,24},{24,32},{32,40},{40,48},{48,56},{56,64},{64,7... | collective-permute-start | bytes 3145736 | tf_op jit(solution)/shard_map/ppermute | solution.py:19
  57.6 25.1 %collective-permute-start.3 = (bf16[512,1024]{1,0:T(8,128)(2,1)S(1)}, bf16[512,1024]{1,0:T(8,128)(2,1)S(1)}, u32[]{:S(2)}, u32[]{:S(2)}) collective-permute-start(bf16[512,1024]{1,0:T(8,128)(2,1)S(1)} %collective-permute-done.1), channel_id=1, source_target_pairs={{0,120},{8,0},{16,8},{24,16},{32,24},{40,32},{48,40},{56,48},{64,5... | collective-permute-start | bytes 3145736 | tf_op jit(solution)/shard_map/ppermute | solution.py:24
  82.7 4.8 %copy-start.2 = (bf16[512,1024]{1,0:T(8,128)(2,1)}, bf16[512,1024]{1,0:T(8,128)(2,1)S(1)}, u32[]{:S(2)}) copy-start(bf16[512,1024]{1,0:T(8,128)(2,1)S(1)} %collective-permute-done.2) | copy-start | bytes 3145732
  82.7 24.2 %collective-permute-start.4 = (bf16[512,1024]{1,0:T(8,128)(2,1)S(1)}, bf16[512,1024]{1,0:T(8,128)(2,1)S(1)}, u32[]{:S(2)}, u32[]{:S(2)}) collective-permute-start(bf16[512,1024]{1,0:T(8,128)(2,1)S(1)} %collective-permute-done.2), channel_id=1, source_target_pairs={{0,8},{8,16},{16,24},{24,32},{32,40},{40,48},{48,56},{56,64},{64,7... | collective-permute-start | bytes 3145736 | tf_op jit(solution)/shard_map/ppermute | solution.py:19
  82.7 70.9 %copy-start.4 = (bf16[512,1024]{1,0:T(8,128)(2,1)}, bf16[512,1024]{1,0:T(8,128)(2,1)S(1)}, u32[]{:S(2)}) copy-start(bf16[512,1024]{1,0:T(8,128)(2,1)S(1)} %collective-permute-done.3) | copy-start | bytes 3145732
  82.7 24.2 %collective-permute-start.5 = (bf16[512,1024]{1,0:T(8,128)(2,1)S(1)}, bf16[512,1024]{1,0:T(8,128)(2,1)S(1)}, u32[]{:S(2)}, u32[]{:S(2)}) collective-permute-start(bf16[512,1024]{1,0:T(8,128)(2,1)S(1)} %collective-permute-done.3), channel_id=1, source_target_pairs={{0,120},{8,0},{16,8},{24,16},{32,24},{40,32},{48,40},{56,48},{64,5... | collective-permute-start | bytes 3145736 | tf_op jit(solution)/shard_map/ppermute | solution.py:24
  106.9 46.8 %copy-start.5 = (bf16[512,1024]{1,0:T(8,128)(2,1)}, bf16[512,1024]{1,0:T(8,128)(2,1)S(1)}, u32[]{:S(2)}) copy-start(bf16[512,1024]{1,0:T(8,128)(2,1)S(1)} %collective-permute-done.4) | copy-start | bytes 3145732
  106.9 23.3 %collective-permute-start.6 = (bf16[512,1024]{1,0:T(8,128)(2,1)S(1)}, bf16[512,1024]{1,0:T(8,128)(2,1)S(1)}, u32[]{:S(2)}, u32[]{:S(2)}) collective-permute-start(bf16[512,1024]{1,0:T(8,128)(2,1)S(1)} %collective-permute-done.4), channel_id=1, source_target_pairs={{0,8},{8,16},{16,24},{24,32},{32,40},{40,48},{48,56},{56,64},{64,7... | collective-permute-start | bytes 3145736 | tf_op jit(solution)/shard_map/ppermute | solution.py:19
  106.9 46.7 %copy-start.3 = (bf16[512,1024]{1,0:T(8,128)(2,1)}, bf16[512,1024]{1,0:T(8,128)(2,1)S(1)}, u32[]{:S(2)}) copy-start(bf16[512,1024]{1,0:T(8,128)(2,1)S(1)} %collective-permute-done.5) | copy-start | bytes 3145732
  106.9 24.3 %collective-permute-start.7 = (bf16[512,1024]{1,0:T(8,128)(2,1)S(1)}, bf16[512,1024]{1,0:T(8,128)(2,1)}, u32[]{:S(2)}, u32[]{:S(2)}) collective-permute-start(bf16[512,1024]{1,0:T(8,128)(2,1)S(1)} %collective-permute-done.5), channel_id=1, source_target_pairs={{0,120},{8,0},{16,8},{24,16},{32,24},{40,32},{48,40},{56,48},{64,5... | collective-permute-start | bytes 3145736 | tf_op jit(solution)/shard_map/ppermute | solution.py:24
  130.2 1.0 copy-start.1
  131.2 22.5 %collective-permute-start.8 = (bf16[512,1024]{1,0:T(8,128)(2,1)S(1)}, bf16[512,1024]{1,0:T(8,128)(2,1)}, u32[]{:S(2)}, u32[]{:S(2)}) collective-permute-start(bf16[512,1024]{1,0:T(8,128)(2,1)S(1)} %collective-permute-done.6), channel_id=1, source_target_pairs={{0,8},{8,16},{16,24},{24,32},{32,40},{40,48},{48,56},{56,64},{64,7... | collective-permute-start | bytes 3145736 | tf_op jit(solution)/shard_map/ppermute | solution.py:19
  131.2 101.3 %collective-permute-start.9 = (bf16[512,1024]{1,0:T(8,128)(2,1)}, bf16[512,1024]{1,0:T(8,128)(2,1)}, u32[]{:S(2)}, u32[]{:S(2)}) collective-permute-start(bf16[512,1024]{1,0:T(8,128)(2,1)} %collective-permute-done.7), channel_id=1, source_target_pairs={{0,120},{8,0},{16,8},{24,16},{32,24},{40,32},{48,40},{56,48},{64,5... | collective-permute-start | bytes 3145736 | tf_op jit(solution)/shard_map/ppermute | solution.py:24
  153.7 83.9 %collective-permute-start.10 = (bf16[512,1024]{1,0:T(8,128)(2,1)}, bf16[512,1024]{1,0:T(8,128)(2,1)}, u32[]{:S(2)}, u32[]{:S(2)}) collective-permute-start(bf16[512,1024]{1,0:T(8,128)(2,1)} %collective-permute-done.8), channel_id=1, source_target_pairs={{0,8},{8,16},{16,24},{24,32},{32,40},{40,48},{48,56},{56,64},{64,7... | collective-permute-start | bytes 3145736 | tf_op jit(solution)/shard_map/ppermute | solution.py:19
  155.0 20.4 %all-to-all-start.1 = ((s32[16,1,1]{2,1,0:T(1,128)}), s32[16,1,1]{2,1,0:T(1,128)S(1)}, u32[]{:S(2)}, u32[]{:S(2)}) async-start(s32[16,1,1]{2,1,0:T(1,128)} %copy.15), calls=%async_computation.1 | async-start | bytes 16384 | tf_op jit(solution)/shard_map/all_to_all | solution.py:49
  175.4 20.0 %all-to-all-start = ((s32[16,1,2]{2,1,0:T(1,128)}), s32[16,1,2]{2,1,0:T(1,128)S(1)}, u32[]{:S(2)}, u32[]{:S(2)}) async-start(s32[16,1,2]{2,1,0:T(1,128)} %copy.14), calls=%async_computation | async-start | bytes 16384 | tf_op jit(solution)/shard_map/all_to_all | solution.py:43
  195.4 23.3 %all-to-all-start.2 = ((s32[16,1,2]{2,1,0:T(1,128)}), s32[16,1,2]{2,1,0:T(1,128)S(1)}, u32[]{:S(2)}, u32[]{:S(2)}) async-start(s32[16,1,2]{2,1,0:T(1,128)} %copy.16), calls=%async_computation.2 | async-start | bytes 16384 | tf_op jit(solution)/shard_map/all_to_all | solution.py:46
  232.5 27.7 %collective-permute-start.11 = (bf16[512,1024]{1,0:T(8,128)(2,1)}, bf16[512,1024]{1,0:T(8,128)(2,1)S(1)}, u32[]{:S(2)}, u32[]{:S(2)}) collective-permute-start(bf16[512,1024]{1,0:T(8,128)(2,1)} %collective-permute-done.9), channel_id=1, source_target_pairs={{0,120},{8,0},{16,8},{24,16},{32,24},{40,32},{48,40},{56,48},{64,5... | collective-permute-start | bytes 3145736 | tf_op jit(solution)/shard_map/ppermute | solution.py:24
  237.6 30.3 %collective-permute-start.12 = (bf16[512,1024]{1,0:T(8,128)(2,1)}, bf16[512,1024]{1,0:T(8,128)(2,1)S(1)}, u32[]{:S(2)}, u32[]{:S(2)}) collective-permute-start(bf16[512,1024]{1,0:T(8,128)(2,1)} %collective-permute-done.10), channel_id=1, source_target_pairs={{0,8},{8,16},{16,24},{24,32},{32,40},{40,48},{48,56},{56,64},{64,7... | collective-permute-start | bytes 3145736 | tf_op jit(solution)/shard_map/ppermute | solution.py:19
  260.2 26.9 %collective-permute-start.13 = (bf16[512,1024]{1,0:T(8,128)(2,1)S(1)}, bf16[512,1024]{1,0:T(8,128)(2,1)S(1)}, u32[]{:S(2)}, u32[]{:S(2)}) collective-permute-start(bf16[512,1024]{1,0:T(8,128)(2,1)S(1)} %collective-permute-done.11), channel_id=1, source_target_pairs={{0,120},{8,0},{16,8},{24,16},{32,24},{40,32},{48,40},{56,48},{64,5... | collective-permute-start | bytes 3145736 | tf_op jit(solution)/shard_map/ppermute | solution.py:24
  267.9 26.7 %collective-permute-start.14 = (bf16[512,1024]{1,0:T(8,128)(2,1)S(1)}, bf16[512,1024]{1,0:T(8,128)(2,1)S(1)}, u32[]{:S(2)}, u32[]{:S(2)}) collective-permute-start(bf16[512,1024]{1,0:T(8,128)(2,1)S(1)} %collective-permute-done.12), channel_id=1, source_target_pairs={{0,8},{8,16},{16,24},{24,32},{32,40},{40,48},{48,56},{56,64},{64,7... | collective-permute-start | bytes 3145736 | tf_op jit(solution)/shard_map/ppermute | solution.py:19
Sparse Core Ops, SparseCore 0:
  31.4 49.5 all-gather.5
